TPU v7x, 32 devices: a whole 2x2x4 slice. The times are simulated.
32 devices in a mesh: run: 1, row: 16 (over z, y, core), col: 1, seg: 2 (over x).
Axes of the slice: x: 2, y: 2, z: 4, core: 2. Of those that a mesh axis runs over, the one named last changes fastest.
Arguments:
- traces: bfloat16 [2, 1024, 2048], P(('run', 'seg'), 'row', 'col'), may hold values from -30 to 30
- live_mask: int32 [1024], P(('run', 'row')), may hold values 0 or 1
- sources: int32 [64], replicated, may hold values from 0 to 1023
- owners: int32 [64, 1], replicated, may hold values from 0 to 15; in each aligned block of 64 rows (0 to 63, 64 to 127, ...) at most 12 rows name the same one
Outputs:
- gathers: bfloat16 [192, 16, 64, 256], P(('run', 'row'), None, ('col', 'seg'))
Inputs may be any that keep to these rules, and one draw needn't show every extreme that they name: `owners`: at most 12 sources share an owner, and some owner has exactly 12.
All inputs are finite; a program needn't handle non-finite values. No bound on the sum of `live_mask` on one device may be relied on, other than what follows from the above.
Results may differ from a plain program's by a relative error of at most 0.024.
Values may be sent and summed in bfloat16 or wider, within the bound.
No kernel may reach another device: no remote copies, remote signals or barrier semaphores. Data moves between devices by JAX's collectives and lax.ppermute only.
A program may use at most 64 MiB of HBM per device.

v0:
```python
import math
import jax
import jax.numpy as jnp
from jax import lax
from jax.sharding import PartitionSpec as P

NT = 2048
NF = 1024
LAGS = 256
BAND = 64
two_pi = 2.0 * math.pi


def turn_table(first_ids, second_ids, period):
    product = first_ids[:, None] * second_ids[None, :] % period
    return product.astype(jnp.float32) * (two_pi / period)


def lag_matrix(bin_ids):
    lag_ids = jnp.arange(LAGS, dtype=jnp.int32) - LAGS // 2 + NT
    lag_angles = turn_table(bin_ids, lag_ids, NT)
    return jnp.concatenate(
        [jnp.cos(lag_angles).astype(jnp.bfloat16), -jnp.sin(lag_angles).astype(jnp.bfloat16)],
        axis=0,
    )


def correlate(recv_real, recv_imag, real_source, imag_source, lag_table):
    cross_real = (
        real_source[:, None, :] * recv_real[:, :, None]
        + imag_source[:, None, :] * recv_imag[:, :, None]
    ).astype(jnp.bfloat16)
    cross_imag = (
        imag_source[:, None, :] * recv_real[:, :, None]
        - real_source[:, None, :] * recv_imag[:, :, None]
    ).astype(jnp.bfloat16)
    stacked_cross = jnp.concatenate([cross_real, cross_imag], axis=0)
    return jnp.einsum("fl,fgv->gvl", lag_table, stacked_cross, preferred_element_type=jnp.float32)


def local(traces, live_mask, sources, owners):
    col_count = lax.axis_size("col")
    seg_count = lax.axis_size("seg")
    row_count = lax.axis_size("row")
    samples = traces[0]
    channels = samples.shape[0]
    local_width = samples.shape[1]
    num_sources = sources.shape[0]
    first_sample = lax.axis_index("col") * local_width
    half_bins = NF // col_count
    sample_ids = first_sample + jnp.arange(local_width, dtype=jnp.int32)
    bin_ids = jnp.arange(half_bins * lax.axis_size("col"), dtype=jnp.int32)
    angles = turn_table(sample_ids, bin_ids, NT)
    cosine = jnp.cos(angles).astype(jnp.bfloat16)
    sine_table = jnp.sin(angles).astype(jnp.bfloat16)
    real_part = jnp.einsum("tf,ct->fc", cosine, samples, preferred_element_type=jnp.float32)
    imag_part = -jnp.einsum("tf,ct->fc", sine_table, samples, preferred_element_type=jnp.float32)
    spectra = lax.psum_scatter(
        jnp.concatenate([real_part, imag_part], axis=1).astype(jnp.bfloat16),
        "col",
        scatter_dimension=0,
        tiled=True,
    ).astype(jnp.float32)
    squares = (spectra * spectra).reshape(half_bins // BAND, BAND, 2, channels)
    band_power = jnp.sum(squares, axis=(1, 2)) / (2 * BAND) + 1e-05
    scaling = live_mask.astype(jnp.float32)[None, :] / jnp.sqrt(band_power)
    scaling = jnp.repeat(scaling, BAND, axis=0)
    whitened = (
        (spectra.reshape(half_bins, 2, channels) * scaling[:, None, :])
        .reshape(half_bins, 2 * channels)
        .astype(jnp.bfloat16)
    )
    white_real = whitened[:, :channels]
    white_imag = whitened[:, channels:]
    everyone = lax.all_gather(whitened, "row", axis=1, tiled=True)
    block_ids = sources // channels
    within = sources % channels
    real_cols = block_ids * (2 * channels) + within
    source_real = jnp.take(everyone, real_cols, axis=1)
    source_imag = jnp.take(everyone, real_cols + channels, axis=1)
    receivers = channels // (col_count * seg_count)
    bin_ids = lax.axis_index("col") * half_bins + jnp.arange(half_bins, dtype=jnp.int32)
    lag_table = lag_matrix(bin_ids)
    real_source = source_real.astype(jnp.float32)
    imag_source = source_imag.astype(jnp.float32)

    def one_group(offset):
        recv_real = lax.dynamic_slice_in_dim(white_real, offset, receivers, 1).astype(jnp.float32)
        recv_imag = lax.dynamic_slice_in_dim(white_imag, offset, receivers, 1).astype(jnp.float32)
        return correlate(recv_real, recv_imag, real_source, imag_source, lag_table)

    offsets = (
        jnp.arange(receivers * lax.axis_size(("col", "seg")) // receivers, dtype=jnp.int32)
        * receivers
    )
    blocks = lax.map(one_group, offsets)
    stacked = lax.psum_scatter(
        blocks.reshape(receivers * lax.axis_size(("col", "seg")), num_sources, LAGS).astype(
            jnp.bfloat16
        ),
        ("col", "seg"),
        scatter_dimension=0,
        tiled=True,
    ).astype(jnp.float32)
    mean_sq = jnp.mean(stacked * stacked, axis=-1, keepdims=True)
    normed = (stacked / jnp.sqrt(mean_sq + 1e-06)).astype(jnp.bfloat16)
    capacity = 3 * num_sources // row_count
    owner_ids = owners[:, 0]
    order_ids = jnp.arange(num_sources, dtype=jnp.int32)
    earlier = (owner_ids[:, None] == owner_ids[None, :]) & (order_ids[None, :] < order_ids[:, None])
    slot_rank = jnp.sum(earlier.astype(jnp.int32), axis=1)
    slot_ids = owner_ids * capacity + slot_rank
    placing = (
        jnp.arange(row_count * capacity, dtype=jnp.int32)[:, None] == slot_ids[None, :]
    ).astype(jnp.bfloat16)
    outgoing = jnp.einsum(
        "sv,gvl->sgl", placing, normed, preferred_element_type=jnp.float32
    ).astype(jnp.bfloat16)
    return lax.all_to_all(outgoing[:, None], "row", split_axis=0, concat_axis=1, tiled=True)


def solution(mesh):
    placed = (P(("run", "seg"), "row", "col"), P(("run", "row")), P(), P())
    return jax.shard_map(
        local,
        mesh=mesh,
        in_specs=placed,
        out_specs=P(("run", "row"), None, ("col", "seg"), None),
        check_vma=False,
    )
```

profile of v0, /device:TPU:1, one launch (start us, length us, event | category | flops | bytes accessed | tf_op | source)
XLA Modules:
  0.0 271.0 jit_solution(1408020758581116476)
XLA Ops:
  6.5 0.9 copy-done
  7.5 31.3 %fusion.21 = bf16[1024,64]{0,1:T(8,128)(2,1)S(1)} fusion(bf16[1,64,2048]{2,1,0:T(8,128)(2,1)S(1)} %copy-done), kind=kOutput, calls=%fused_computation.35 | convolution fusion | flops 300023808 | bytes 393216 | tf_op jit(solution)/shard_map/tf,ct->fc/dot_general | solution.py:57
  38.8 31.2 %fusion.22 = bf16[1024,64]{0,1:T(8,128)(2,1)S(1)} fusion(bf16[1,64,2048]{2,1,0:T(8,128)(2,1)S(1)} %copy-done), kind=kOutput, calls=%fused_computation.36 | convolution fusion | flops 299958272 | bytes 393216 | tf_op jit(solution)/shard_map/tf,ct->fc/dot_general | solution.py:56
  70.1 0.3 mul.149
  70.4 0.2 reduce_sum.28
  70.7 0.1 copy.16
  70.8 0.2 broadcast_in_dim.19
  71.0 0.2 mul.150
  71.2 0.8 multiply_convert_fusion
  72.1 1.0 fusion.48
  73.1 4.2 %cosine_convert_fusion.4 = bf16[1024,256]{1,0:T(8,128)(2,1)S(1)} fusion(s32[256]{0:T(256)S(1)} %iota_add_fusion), kind=kLoop, calls=%fused_computation.43 | loop fusion | flops 3932160 | bytes 525312 | tf_op jit(solution)/shard_map/convert_element_type | solution.py:23
  77.3 4.0 %fusion.31 = bf16[1024,256]{1,0:T(8,128)(2,1)S(1)} fusion(s32[256]{0:T(256)S(1)} %iota_add_fusion), kind=kLoop, calls=%fused_computation.47 | loop fusion | flops 4718592 | bytes 525312 | tf_op jit(solution)/shard_map/neg | solution.py:23
  81.4 1.0 pad_maximum_fusion
  82.4 42.7 %all-gather.2.cloned.1.call-done = bf16[1024,2048]{0,1:T(8,128)(2,1)} async-done(((bf16[1024,128]{0,1:T(8,128)(2,1)}), bf16[1024,2048]{0,1:T(8,128)(2,1)}) %all-gather.2.cloned.1.call-update) | async-done | bytes 4194320 | tf_op jit(solution)/shard_map/all_gather | solution.py:75
  125.1 3.5 %gather_fusion = bf16[64,1024]{1,0:T(8,128)(2,1)S(1)} fusion(bf16[1024,2048]{0,1:T(8,128)(2,1)} %all-gather.2.cloned.1.call-done, s32[1024]{0:T(1024)S(1)} %pad_clamp_fusion.1), kind=kCustom, calls=%fused_computation.clone | custom fusion | bytes 262400 | tf_op jit(solution)/shard_map/jit(_take)/gather | solution.py:79
  128.6 3.5 %gather_fusion.1 = bf16[64,1024]{1,0:T(8,128)(2,1)S(1)} fusion(bf16[1024,2048]{0,1:T(8,128)(2,1)} %all-gather.2.cloned.1.call-done, s32[1024]{0:T(1024)S(1)} %pad_clamp_fusion), kind=kCustom, calls=%fused_computation.1.clone | custom fusion | bytes 262400 | tf_op jit(solution)/shard_map/jit(_take)/gather | solution.py:80
  132.2 0.1 bitcast_convert_fusion
  132.3 16.3 %while.10 = (s32[]{:T(128)}, bf16[2,32,64,256]{3,2,1,0:T(8,128)(2,1)S(1)}, f32[1024,64]{0,1:T(8,128)S(1)}, s32[2]{0:T(128)S(1)}, bf16[1024,64]{0,1:T(8,128)(2,1)...) while((s32[]{:T(128)}, ...), condition=%wide.region_3.5_spmd, body=%wide.region_2.4_spmd.sunk | while | flops 2181103616 | bytes 25297088 | solution.py:96
  132.3 0.7 dynamic_slice.15
  135.1 2.8 %add_convert_fusion.2 = (bf16[1024,32,64]{0,2,1:T(8,128)(2,1)S(1)}, bf16[1024,32,64]{0,2,1:T(8,128)(2,1)S(1)}) fusion(f32[1024,32]{0,1:T(8,128)S(1)} %get-tuple-element.129, f32[1024,64]{0,1:T(8,128)S(1)} %get-tuple-element.160, f32[1024,32]{0,1:T(8,128)S(1)} %get-tuple-element.130, f32[1024,64]{0,1:T(8,128)S(1)} %get-tuple-element.157), kind=kLoop, calls=%fused_computation.7.clone.1 | loop fusion | flops 16777216 | bytes 9175040 | tf_op jit(solution)/shard_map/while/body/eval_jaxpr/convert_element_type | solution.py:32
  137.9 2.5 bitcast_dynamic-update-slice_fusion.2
  140.5 0.7 dynamic_slice.15
  143.3 2.8 %add_convert_fusion.2 = (bf16[1024,32,64]{0,2,1:T(8,128)(2,1)S(1)}, bf16[1024,32,64]{0,2,1:T(8,128)(2,1)S(1)}) fusion(f32[1024,32]{0,1:T(8,128)S(1)} %get-tuple-element.129, f32[1024,64]{0,1:T(8,128)S(1)} %get-tuple-element.160, f32[1024,32]{0,1:T(8,128)S(1)} %get-tuple-element.130, f32[1024,64]{0,1:T(8,128)S(1)} %get-tuple-element.157), kind=kLoop, calls=%fused_computation.7.clone.1 | loop fusion | flops 16777216 | bytes 9175040 | tf_op jit(solution)/shard_map/while/body/eval_jaxpr/convert_element_type | solution.py:32
  146.1 2.5 bitcast_dynamic-update-slice_fusion.2
  148.7 1.3 copy-done.1
  150.0 0.2 convert_reduce_fusion
  150.2 29.8 %reduce-scatter.2.cloned.1.call-done = bf16[32,64,256]{2,1,0:T(8,128)(2,1)} async-done(((bf16[64,64,256]{2,1,0:T(8,128)(2,1)}), bf16[32,64,256]{2,1,0:T(8,128)(2,1)}) %reduce-scatter.2.cloned.1.call-update) | async-done | bytes 1048592 | tf_op jit(solution)/shard_map/reduce_scatter | solution.py:97
  180.0 1.6 fusion.18
  181.6 2.3 convert_bitcast_fusion
  184.0 1.8 copy.17
  185.7 76.3 %all_to_all.18 = bf16[192,1,32,256]{3,2,1,0:T(8,128)(2,1)S(1)} all-to-all(bf16[192,1,32,256]{3,2,1,0:T(8,128)(2,1)S(1)} %copy.17), channel_id=1, replica_groups=mesh['run'=1,'row'=16,'col'=1,'seg'=2] {'row'}, dimensions={0} | all-to-all | bytes 6291456 | tf_op jit(solution)/shard_map/all_to_all | solution.py:119
  262.1 2.1 copy.18
  (32 shorter events, 0.4 us)
Async XLA Ops:
  6.5 1.0 copy-start
  6.5 118.6 %all-gather.2.cloned.1.call-start = ((), (), s32[]{:S(2)}) async-start(), calls=%async_computation.2 | async-start | bytes 4456448 | tf_op jit(solution)/shard_map/all_gather | solution.py:75
  38.8 31.9 %copy-start.4 = (s32[64]{0:T(128)S(1)}, s32[64]{0:T(128)}, u32[]{:S(2)}) copy-start(s32[64]{0:T(128)} %param.9) | copy-start | bytes 772
  70.1 2.0 copy-start.3
  72.0 108.0 %reduce-scatter.2.cloned.1.call-start = ((), (), s32[]{:S(2)}) async-start(), calls=%async_computation.3 | async-start | bytes 3145728 | tf_op jit(solution)/shard_map/reduce_scatter | solution.py:97
  132.3 17.7 %copy-start.5 = (s32[64,1]{0,1:T(1,128)S(1)}, s32[64,1]{0,1:T(1,128)}, u32[]{:S(2)}) copy-start(s32[64,1]{0,1:T(1,128)} %param.11) | copy-start | bytes 772
  135.1 2.8 %copy-start.2 = (bf16[2048,256]{1,0:T(8,128)(2,1)S(1)}, bf16[2048,256]{1,0:T(8,128)(2,1)}, u32[]{:S(2)}) copy-start(bf16[2048,256]{1,0:T(8,128)(2,1)} %get-tuple-element.162) | copy-start | bytes 3145732 | tf_op jit(solution)/shard_map/while
  143.3 2.8 %copy-start.2 = (bf16[2048,256]{1,0:T(8,128)(2,1)S(1)}, bf16[2048,256]{1,0:T(8,128)(2,1)}, u32[]{:S(2)}) copy-start(bf16[2048,256]{1,0:T(8,128)(2,1)} %get-tuple-element.162) | copy-start | bytes 3145732 | tf_op jit(solution)/shard_map/while
  148.7 1.3 copy-start.1
Sparse Core Ops, SparseCore 0:
  72.1 52.9 all-gather.1
  150.1 29.8 reduce-scatter.1
where the time goes:
time: 271 us
  blocking collectives  76.3 us (28%)
  waiting for transfers between devices  72.6 us (27%)
  matrix products  70 us (26%)
  other arithmetic  17.9 us (7%)
  local copies, waits for them, and re-layouts  16.3 us (6%)
  between operations  13.6 us (5%)
  loops' own time  4.26 us (2%)
    all_to_all x1, blocking collectives, local(): lax.all_to_all(outgoing[:, None], 'row', split_axis=0, concat_axis=1, til...  76.3 us
    all_gather x1, waiting for transfers between devices, local(): everyone = lax.all_gather(whitened, 'row', axis=1, tiled=True)  42.7 us
    dot_general x1, matrix products, local(): jnp.einsum('tf,ct->fc', sine_table, samples, preferred_element_type=jnp.f...  31.3 us
    dot_general x1, matrix products, local(): jnp.einsum('tf,ct->fc', cosine, samples, preferred_element_type=jnp.float32)  31.2 us
    reduce_scatter x1, waiting for transfers between devices, local(): lax.psum_scatter(blocks.reshape(receivers * lax.axis_size(('col', 'seg'))...  29.8 us
    convert_element_type x2, other arithmetic, correlate(): cross_real = (real_source[:, None, :] * recv_real[:, :, None] + imag_sour...  5.58 us
  transfers between devices with their start and end apart: 2, of which 2 were waited for; matrix products, arithmetic and copies ran while one was open for 4% of the time, Pallas kernels for 0%

commit v1 on v0

--- a/solution.py
+++ b/solution.py
@@ -72,7 +72,14 @@
     )
     white_real = whitened[:, :channels]
     white_imag = whitened[:, channels:]
-    everyone = lax.all_gather(whitened, "row", axis=1, tiled=True)
+    ways, here = (lax.axis_size("row"), lax.axis_index("row"))
+    everyone, reach = (whitened, 1)
+    while reach < ways:
+        theirs = lax.ppermute(everyone, "row", [(d, d ^ reach) for d in range(ways)])
+        mine_first = jnp.concatenate([everyone, theirs], axis=1)
+        theirs_first = jnp.concatenate([theirs, everyone], axis=1)
+        everyone = jnp.where(here & reach == 0, mine_first, theirs_first)
+        reach = 2 * reach
     block_ids = sources // channels
     within = sources % channels
     real_cols = block_ids * (2 * channels) + within

time: 271 us -> 361 us (1.33)
  waiting for transfers between devices: 72.6 us -> 150 us
  other arithmetic: 17.9 us -> 25.2 us
  starting transfers between devices: 0.04 us -> 5.85 us
    ppermute x0 -> x4, waiting for transfers between devices: none -> 117 us  [local(): lax.ppermute(everyone, 'row', [(d, d ^ reach) for d in range(ways)])]
    all_gather x1 -> x0, waiting for transfers between devices: 42.7 us -> none  [local(): everyone = lax.all_gather(whitened, 'row', axis=1, tiled=True)]
    select_n x0 -> x4, other arithmetic: none -> 8.03 us  [local(): everyone = jnp.where(here & reach == 0, mine_first, theirs_first)]
    ppermute x0 -> x4, starting transfers between devices: none -> 5.84 us  [local(): lax.ppermute(everyone, 'row', [(d, d ^ reach) for d in range(ways)])]
  transfers between devices with their start and end apart: 2 -> 5, of which waited for: 2 -> 5; matrix products, arithmetic and copies ran while one was open for 4% -> 3% of each run, Pallas kernels for 0% -> 0%
where the time goes in v1:
time: 361 us
  waiting for transfers between devices  150 us (42%)
  blocking collectives  76.3 us (21%)
  matrix products  70 us (19%)
  other arithmetic  25.2 us (7%)
  local copies, waits for them, and re-layouts  16.3 us (5%)
  between operations  13.7 us (4%)
  starting transfers between devices  5.85 us (2%)
  loops' own time  3.99 us (1%)
    ppermute x4, waiting for transfers between devices, local(): lax.ppermute(everyone, 'row', [(d, d ^ reach) for d in range(ways)])  117 us
    all_to_all x1, blocking collectives, local(): lax.all_to_all(outgoing[:, None], 'row', split_axis=0, concat_axis=1, til...  76.3 us
    reduce_scatter x1, waiting for transfers between devices, local(): lax.psum_scatter(blocks.reshape(receivers * lax.axis_size(('col', 'seg'))...  33 us
    dot_general x1, matrix products, local(): jnp.einsum('tf,ct->fc', sine_table, samples, preferred_element_type=jnp.f...  31.3 us
    dot_general x1, matrix products, local(): jnp.einsum('tf,ct->fc', cosine, samples, preferred_element_type=jnp.float32)  31.2 us
    select_n x4, other arithmetic, local(): everyone = jnp.where(here & reach == 0, mine_first, theirs_first)  8.03 us
  transfers between devices with their start and end apart: 5, of which 5 were waited for; matrix products, arithmetic and copies ran while one was open for 3% of the time, Pallas kernels for 0%

profile of v1, /device:TPU:1, one launch (start us, length us, event | category | flops | bytes accessed | tf_op | source)
XLA Modules:
  0.0 360.9 jit_solution(9962822500371504599)
XLA Ops:
  6.5 0.9 copy-done
  7.5 31.3 %fusion.21 = bf16[1024,64]{0,1:T(8,128)(2,1)S(1)} fusion(bf16[1,64,2048]{2,1,0:T(8,128)(2,1)S(1)} %copy-done), kind=kOutput, calls=%fused_computation.37 | convolution fusion | flops 300023808 | bytes 393216 | tf_op jit(solution)/shard_map/tf,ct->fc/dot_general | solution.py:57
  38.8 31.2 %fusion.22 = bf16[1024,64]{0,1:T(8,128)(2,1)S(1)} fusion(bf16[1,64,2048]{2,1,0:T(8,128)(2,1)S(1)} %copy-done), kind=kOutput, calls=%fused_computation.38 | convolution fusion | flops 299958272 | bytes 393216 | tf_op jit(solution)/shard_map/tf,ct->fc/dot_general | solution.py:56
  71.3 1.5 collective-permute-done
  73.0 2.4 collective-permute-start.1
  75.4 11.9 %collective-permute-done.1 = bf16[1024,256]{0,1:T(8,128)(2,1)S(1)} collective-permute-done((bf16[1024,256]{0,1:T(8,128)(2,1)S(1)}, bf16[1024,256]{0,1:T(8,128)(2,1)S(1)}, u32[]{:S(2)}, u32[]{:S(2)}) %collective-permute-start.1) | collective-permute-done | bytes 524320 | tf_op jit(solution)/shard_map/ppermute | solution.py:78
  87.8 1.3 collective-permute-start.2
  89.1 22.6 %collective-permute-done.2 = bf16[1024,512]{0,1:T(8,128)(2,1)} collective-permute-done((bf16[1024,512]{0,1:T(8,128)(2,1)S(1)}, bf16[1024,512]{0,1:T(8,128)(2,1)}, u32[]{:S(2)}, u32[]{:S(2)}) %collective-permute-start.2) | collective-permute-done | bytes 1048608 | tf_op jit(solution)/shard_map/ppermute | solution.py:78
  111.8 2.5 maximum_select_fusion.1
  114.3 2.0 collective-permute-start.3
  116.4 1.0 fusion.48
  117.4 4.0 %cosine_convert_fusion.4 = bf16[1024,256]{1,0:T(8,128)(2,1)S(1)} fusion(s32[256]{0:T(256)S(1)} %iota_add_fusion), kind=kLoop, calls=%fused_computation.46 | loop fusion | flops 3932160 | bytes 525312 | tf_op jit(solution)/shard_map/convert_element_type | solution.py:23
  121.4 4.2 %fusion.31 = bf16[1024,256]{1,0:T(8,128)(2,1)S(1)} fusion(s32[256]{0:T(256)S(1)} %iota_add_fusion), kind=kLoop, calls=%fused_computation.50 | loop fusion | flops 4718592 | bytes 525312 | tf_op jit(solution)/shard_map/neg | solution.py:23
  125.6 1.1 pad_maximum_fusion
  126.7 80.5 %collective-permute-done.3 = bf16[1024,1024]{0,1:T(8,128)(2,1)} collective-permute-done((bf16[1024,1024]{0,1:T(8,128)(2,1)S(1)}, bf16[1024,1024]{0,1:T(8,128)(2,1)}, u32[]{:S(2)}, u32[]{:S(2)}) %collective-permute-start.3) | collective-permute-done | bytes 2097184 | tf_op jit(solution)/shard_map/ppermute | solution.py:78
  207.2 4.9 %maximum_select_fusion = bf16[1024,2048]{0,1:T(8,128)(2,1)} fusion(bf16[1024,1024]{0,1:T(8,128)(2,1)} %collective-permute-done.3, bf16[1024,1024]{0,1:T(8,128)(2,1)S(1)} %maximum_select_fusion.1, pred[]{:T(512)S(6)} %eq.50), kind=kLoop, calls=%fused_computation.26 | loop fusion | flops 18874368 | bytes 8388609 | tf_op jit(solution)/shard_map/jit(_where)/select_n | solution.py:81
  212.1 3.7 %gather_fusion = bf16[64,1024]{1,0:T(8,128)(2,1)S(1)} fusion(bf16[1024,2048]{0,1:T(8,128)(2,1)} %maximum_select_fusion, s32[1024]{0:T(1024)S(1)} %pad_clamp_fusion.1), kind=kCustom, calls=%fused_computation.clone | custom fusion | bytes 262400 | tf_op jit(solution)/shard_map/jit(_take)/gather | solution.py:86
  215.8 3.5 gather_fusion.1
  219.4 15.9 %while.10 = (s32[]{:T(128)}, bf16[2,32,64,256]{3,2,1,0:T(8,128)(2,1)S(1)}, f32[1024,64]{0,1:T(8,128)S(1)}, s32[2]{0:T(128)S(1)}, bf16[1024,64]{0,1:T(8,128)(2,1)...) while((s32[]{:T(128)}, ...), condition=%wide.region_3.5_spmd, body=%wide.region_2.4_spmd.sunk | while | flops 2181103616 | bytes 25297088 | solution.py:103
  219.5 0.6 dynamic_slice.15
  222.0 2.8 add_convert_fusion.2
  224.9 2.5 bitcast_dynamic-update-slice_fusion.2
  227.4 0.6 dynamic_slice.15
  230.0 2.8 add_convert_fusion.2
  232.8 2.5 bitcast_dynamic-update-slice_fusion.2
  235.4 1.3 copy-done.3
  236.9 33.0 %reduce-scatter.2.cloned.1.call-done = bf16[32,64,256]{2,1,0:T(8,128)(2,1)} async-done(((bf16[64,64,256]{2,1,0:T(8,128)(2,1)}), bf16[32,64,256]{2,1,0:T(8,128)(2,1)}) %reduce-scatter.2.cloned.1.call-update) | async-done | bytes 1048592 | tf_op jit(solution)/shard_map/reduce_scatter | solution.py:104
  269.9 1.6 fusion.18
  271.5 2.3 convert_bitcast_fusion
  273.8 1.8 copy.17
  275.6 76.3 %all_to_all.18 = bf16[192,1,32,256]{3,2,1,0:T(8,128)(2,1)S(1)} all-to-all(bf16[192,1,32,256]{3,2,1,0:T(8,128)(2,1)S(1)} %copy.17), channel_id=1, replica_groups=mesh['run'=1,'row'=16,'col'=1,'seg'=2] {'row'}, dimensions={0} | all-to-all | bytes 6291456 | tf_op jit(solution)/shard_map/all_to_all | solution.py:126
  352.0 2.1 copy.18
  (45 shorter events, 2.3 us)
Async XLA Ops:
  6.5 1.0 copy-start
  6.5 263.4 %reduce-scatter.2.cloned.1.call-start = ((), (), s32[]{:S(2)}) async-start(), calls=%async_computation.2 | async-start | bytes 3145728 | tf_op jit(solution)/shard_map/reduce_scatter | solution.py:104
  38.8 31.9 %copy-start.6 = (s32[64]{0:T(128)S(1)}, s32[64]{0:T(128)}, u32[]{:S(2)}) copy-start(s32[64]{0:T(128)} %param.9) | copy-start | bytes 772
  71.2 45.2 %copy-start.5 = (s32[64]{0:T(128)S(1)}, s32[64]{0:T(128)}, u32[]{:S(2)}) copy-start(s32[64]{0:T(128)} %param.10) | copy-start | bytes 772
  71.2 17.9 %copy-start.1 = (bf16[1024,2,64]{0,2,1:T(8,128)(2,1)}, bf16[1024,2,64]{0,2,1:T(8,128)(2,1)S(1)}, u32[]{:S(2)}) copy-start(bf16[1024,2,64]{0,2,1:T(8,128)(2,1)S(1)} %multiply_convert_fusion) | copy-start | bytes 786436
  71.3 1.6 collective-permute-start
  73.0 14.4 %collective-permute-start.1 = (bf16[1024,256]{0,1:T(8,128)(2,1)S(1)}, bf16[1024,256]{0,1:T(8,128)(2,1)S(1)}, u32[]{:S(2)}, u32[]{:S(2)}) collective-permute-start(bf16[1024,256]{0,1:T(8,128)(2,1)S(1)} %maximum_select_fusion.3), channel_id=1, source_target_pairs={{0,4},{2,6},{4,0},{6,2},{8,12},{10,14},{12,8},{14,10},{16,20},{18,... | collective-permute-start | bytes 1572872 | tf_op jit(solution)/shard_map/ppermute | solution.py:78
  87.8 23.9 %collective-permute-start.2 = (bf16[1024,512]{0,1:T(8,128)(2,1)S(1)}, bf16[1024,512]{0,1:T(8,128)(2,1)}, u32[]{:S(2)}, u32[]{:S(2)}) collective-permute-start(bf16[1024,512]{0,1:T(8,128)(2,1)S(1)} %maximum_select_fusion.2), channel_id=1, source_target_pairs={{0,8},{2,10},{4,12},{6,14},{8,0},{10,2},{12,4},{14,6},{16,24},{18,... | collective-permute-start | bytes 3145736 | tf_op jit(solution)/shard_map/ppermute | solution.py:78
  114.3 92.9 %collective-permute-start.3 = (bf16[1024,1024]{0,1:T(8,128)(2,1)S(1)}, bf16[1024,1024]{0,1:T(8,128)(2,1)}, u32[]{:S(2)}, u32[]{:S(2)}) collective-permute-start(bf16[1024,1024]{0,1:T(8,128)(2,1)S(1)} %maximum_select_fusion.1), channel_id=1, source_target_pairs={{0,16},{2,18},{4,20},{6,22},{8,24},{10,26},{12,28},{14,30},{16,0},... | collective-permute-start | bytes 6291464 | tf_op jit(solution)/shard_map/ppermute | solution.py:78
  212.1 7.3 %copy-start.2 = (bf16[2,32,64,256]{3,2,1,0:T(8,128)(2,1)S(1)}, bf16[2,32,64,256]{3,2,1,0:T(8,128)(2,1)}, u32[]{:S(2)}) copy-start(bf16[2,32,64,256]{3,2,1,0:T(8,128)(2,1)} %custom-call.4) | copy-start | bytes 6291460
  219.4 17.3 %copy-start.7 = (s32[64,1]{0,1:T(1,128)S(1)}, s32[64,1]{0,1:T(1,128)}, u32[]{:S(2)}) copy-start(s32[64,1]{0,1:T(1,128)} %param.11) | copy-start | bytes 772
  222.0 2.8 copy-start.4
  230.0 2.8 copy-start.4
  235.4 1.3 copy-start.3
Sparse Core Ops, SparseCore 0:
  236.8 33.0 reduce-scatter.1
